TPU v7x, 32 devices: a whole 2x2x4 slice. The times are simulated.
32 devices in a mesh: groups: 2 (over x), day: 16 (over z, y, core).
Axes of the slice: x: 2, y: 2, z: 4, core: 2. Of those that a mesh axis runs over, the one named last changes fastest.
Arguments:
- couplings: float32 [6, 128, 32, 512], P(None, ('groups', 'day')), parts along dimension 1, may hold values from 0.01 to 2.7, as said below
- probe_bits: int32 [16, 128, 32, 512], P(None, ('groups', 'day')), parts along dimension 1, may hold values 0 or 1
- land_mask: int32 [64, 512], P('groups'), parts along dimension 0, may hold values 0 or 1
Outputs:
- variance: float32 [128, 32, 512], P(('groups', 'day')), parts along dimension 0
There are 2 independent parts, one for each index of `groups`. A program takes and returns all parts, laid end to end along the dimension named above; each array names one. Nothing has to cross between parts.
Inputs may be any that keep to these rules, and one draw needn't show every extreme that they name: `couplings`: all weights positive.
All inputs are finite; a program needn't handle non-finite values. No bound on the sum of `probe_bits` on one device may be relied on, other than what follows from the above.
Results may differ from a plain program's by a relative error of at most 0.0003.
Values sent between devices are 32-bit elements; how exact they have to be, the bound alone decides.
No kernel may reach another device: no remote copies, remote signals or barrier semaphores. Data moves between devices by JAX's collectives and lax.ppermute only.
A program may use at most 64 MiB of HBM per device.

v0:
```python
import jax
import jax.numpy as jnp
from jax import lax
from jax.sharding import PartitionSpec as P

ITERS = 3
LINK_OFFSETS = ((0, 1), (1, 0), (1, 1), (1, -1))
COASTAL_FACTOR = 0.2


def passed_along(value, axis, steps):
    count = lax.axis_size(axis)
    pairs = [(source, (source + steps) % count) for source in range(count)]
    return lax.ppermute(value, axis, pairs)


def extended(block, sides, width):
    for axis, dim in sides:
        count = lax.axis_size(axis)
        forward = [(i, i + 1) for i in range(count - 1)]
        forward.append((count - 1, 0))
        backward = [(target, source) for source, target in forward]
        low = lax.ppermute(
            lax.slice_in_dim(block, block.shape[dim] - width, None, axis=dim), axis, forward
        )
        high = lax.ppermute(lax.slice_in_dim(block, 0, width, axis=dim), axis, backward)
        block = jnp.concatenate([low, block, high], axis=dim)
    return block


def shift_plane(values, step_row, step_col):
    lat_size, lon_size = (values.shape[-2], values.shape[-1])
    margins = [(0, 0)] * (values.ndim - 2) + [
        (max(step_row, 0), max(-step_row, 0)),
        (max(step_col, 0), max(-step_col, 0)),
    ]
    padded = jnp.pad(values, margins)
    row_start = max(-step_row, 0)
    col_start = max(-step_col, 0)
    return padded[..., row_start : row_start + lat_size, col_start : col_start + lon_size]


def prepare(couplings, land_mask):
    ones_field = jnp.ones(land_mask.shape, jnp.float32)
    result = [couplings[0]]
    for slot_n, (step_row, step_col) in enumerate(LINK_OFFSETS):
        target = shift_plane(land_mask, -step_row, -step_col)
        inside = shift_plane(ones_field, -step_row, -step_col)
        factor = (
            jnp.where(land_mask == target, jnp.float32(1.0), jnp.float32(COASTAL_FACTOR)) * inside
        )
        result.append(couplings[slot_n + 1] * factor)
    result.append(couplings[5])
    return jnp.stack(result)


def stencil(padded, coef_block, link_prev):
    field = padded[..., 1:-1, :, :]
    next_day = padded[..., 2:, :, :]
    prev_day = padded[..., :-2, :, :]
    result = (
        coef_block[0] * field + coef_block[5] * (field - next_day) + link_prev * (field - prev_day)
    )
    for slot_n, (step_row, step_col) in enumerate(LINK_OFFSETS):
        link_coef = coef_block[slot_n + 1]
        link_back = shift_plane(link_coef, step_row, step_col)
        result = result + link_coef * (field - shift_plane(field, -step_row, -step_col))
        result = result + link_back * (field - shift_plane(field, step_row, step_col))
    return result


def diagonal(coef_block, link_prev):
    result = coef_block[0] + coef_block[5] + link_prev
    for slot_n, (step_row, step_col) in enumerate(LINK_OFFSETS):
        link_coef = coef_block[slot_n + 1]
        result = result + link_coef + shift_plane(link_coef, step_row, step_col)
    return result


def spread(vector):
    return vector[:, None, None, None]


def summed(first, second):
    return jnp.sum(first * second, axis=(1, 2, 3))


def norm_sum(residual, scaled):
    return lax.psum(summed(residual, scaled), "day")


def body(couplings, probe_bits, land_mask):
    probes_n, days_n = (probe_bits.shape[0], probe_bits.shape[1])
    links_eff = prepare(couplings, land_mask)
    signs = (2 * probe_bits - 1).astype(jnp.float32)
    prev_plane = passed_along(links_eff[5, days_n - 1 : days_n], "day", 1)
    link_prev = jnp.concatenate([prev_plane, links_eff[5, : days_n - 1]], axis=0)
    diag_own = diagonal(links_eff, link_prev)
    residual = signs
    scaled = signs / diag_own
    estimate = jnp.zeros_like(signs)
    norm_now = norm_sum(residual, scaled)
    direction = scaled
    for turn in range(ITERS):
        padded = extended(direction, (("day", 1),), 1)
        image = stencil(padded, links_eff, link_prev)
        step_len = norm_now / lax.psum(summed(direction, image), "day")
        estimate = estimate + spread(step_len) * direction
        if turn + 1 < ITERS:
            residual = residual - spread(step_len) * image
            scaled = residual / diag_own
            norm_next = norm_sum(residual, scaled)
            direction = scaled + spread(norm_next / norm_now) * direction
            norm_now = norm_next
    return jnp.sum(signs * estimate, axis=0) / probes_n


def solution(mesh):
    return jax.shard_map(
        body,
        mesh=mesh,
        in_specs=(
            P(None, ("groups", "day"), None, None),
            P(None, ("groups", "day"), None, None),
            P("groups", None),
        ),
        out_specs=P(("groups", "day"), None, None),
        check_vma=False,
    )
```

profile of v0, /device:TPU:0, one launch (start us, length us, event | category | flops | bytes accessed | tf_op | source)
XLA Modules:
  0.0 300.4 jit_solution(4284825563196142856)
XLA Ops:
  0.0 0.0 copy-start
  0.0 1.0 slice_bitcast_fusion.3
  1.0 0.5 collective-permute-start
  1.5 1.2 fusion.93
  2.7 1.3 bitcast_multiply_fusion.3
  4.0 0.9 slice_bitcast_fusion.2
  4.9 3.5 %collective-permute-done = f32[1,32,512]{2,1,0:T(8,128)S(1)} collective-permute-done((f32[1,32,512]{2,1,0:T(8,128)S(1)}, f32[1,32,512]{2,1,0:T(8,128)S(1)}, u32[]{:S(2)}, u32[]{:S(2)}) %collective-permute-start) | collective-permute-done | bytes 65568 | tf_op jit(solution)/shard_map/ppermute | solution.py:14
  8.4 1.5 pad_maximum_fusion.6
  9.9 0.0 copy-done
  9.9 0.9 convert_divide_fusion
  10.8 0.0 copy-start.3
  10.9 0.2 fusion.104
  11.0 1.8 collective-permute-start.1
  12.9 0.0 collective-permute-start.2
  12.9 0.0 copy-done.3
  12.9 0.2 slice_bitcast_fusion.1
  13.1 12.1 %collective-permute-done.1 = f32[16,1,32,512]{3,2,1,0:T(8,128)S(1)} collective-permute-done((f32[16,1,32,512]{3,2,1,0:T(8,128)S(1)}, f32[16,1,32,512]{3,2,1,0:T(8,128)S(1)}, u32[]{:S(2)}, u32[]{:S(2)}) %collective-permute-start.1) | collective-permute-done | bytes 1048608 | tf_op jit(solution)/shard_map/ppermute | solution.py:26
  25.2 4.7 %collective-permute-done.2 = f32[16,1,32,512]{3,2,1,0:T(8,128)S(1)} collective-permute-done((f32[16,1,32,512]{3,2,1,0:T(8,128)S(1)}, f32[16,1,32,512]{3,2,1,0:T(8,128)S(1)}, u32[]{:S(2)}, u32[]{:S(2)}) %collective-permute-start.2) | collective-permute-done | bytes 1048608 | tf_op jit(solution)/shard_map/ppermute | solution.py:23
  29.9 12.8 %multiply_reduce_fusion.4 = (f32[16]{0:T(128)S(1)}, f32[16]{0:T(128)S(1)}, f32[16,4,32,512]{3,2,1,0:T(8,128)}) fusion(f32[4,32,512]{2,1,0:T(8,128)S(1)} %get-tuple-element.31, s32[16,4,32,512]{3,2,1,0:T(8,128)S(1)} %copy-done, f32[16,4,32,512]{3,2,1,0:T(8,128)S(1)} %convert_divide_fusion, f32[4,32,512]{2,1,0:T(8,128)S(1)} %get-tuple-element.35, ...), kind=kLoop, calls=%fused_computation.129 | loop fusion | flops 42991584 | bytes 17825920 | tf_op jit(solution)/shard_map/reduce_sum | solution.py:85
  42.7 35.4 %all-reduce.36 = (f32[16]{0:T(128)S(1)}, f32[16]{0:T(128)S(1)}) all-reduce(f32[16]{0:T(128)S(1)} %get-tuple-element.6, f32[16]{0:T(128)S(1)} %get-tuple-element.5), channel_id=1, replica_groups=mesh['groups'=2,'day'=16] {'day'}, use_global_device_ids=true, to_apply=%region_1.2 | all-reduce | flops 32 | bytes 256 | tf_op jit(solution)/shard_map/psum | solution.py:89
  78.1 6.6 %multiply_reduce_fusion.3 = (f32[16]{0:T(128)S(1)}, f32[16,4,32,512]{3,2,1,0:T(8,128)}) fusion(f32[4,32,512]{2,1,0:T(8,128)S(1)} %get-tuple-element.31, f32[16,4,32,512]{3,2,1,0:T(8,128)} %get-tuple-element.13, f32[16]{0:T(128)S(1)} %div.43, s32[16,4,32,512]{3,2,1,0:T(8,128)} %param.4), kind=kLoop, calls=%fused_computation.127 | loop fusion | flops 8388592 | bytes 12845184 | tf_op jit(solution)/shard_map/reduce_sum | solution.py:85
  84.7 29.6 %psum.44 = f32[16]{0:T(128)S(1)} all-reduce(f32[16]{0:T(128)S(1)} %get-tuple-element.11), channel_id=1, replica_groups=mesh['groups'=2,'day'=16] {'day'}, use_global_device_ids=true, to_apply=%region_5.6 | all-reduce | flops 16 | bytes 128 | tf_op jit(solution)/shard_map/psum | solution.py:89
  114.4 4.6 %multiply_add_fusion.1 = f32[16,4,32,512]{3,2,1,0:T(8,128)S(1)} fusion(f32[16,4,32,512]{3,2,1,0:T(8,128)} %get-tuple-element.12, f32[16]{0:T(128)S(1)} %div.45, f32[4,32,512]{2,1,0:T(8,128)S(1)} %get-tuple-element.31, s32[16,4,32,512]{3,2,1,0:T(8,128)} %param.4), kind=kLoop, calls=%fused_computation.126 | loop fusion | flops 7340032 | bytes 12845120 | tf_op jit(solution)/shard_map/add | solution.py:113
  119.0 0.0 copy-start.1
  119.0 0.3 fusion.103
  119.3 0.1 collective-permute-start.3
  119.4 0.5 collective-permute-start.4
  119.9 11.8 %collective-permute-done.3 = f32[16,1,32,512]{3,2,1,0:T(8,128)S(1)} collective-permute-done((f32[16,1,32,512]{3,2,1,0:T(8,128)S(1)}, f32[16,1,32,512]{3,2,1,0:T(8,128)S(1)}, u32[]{:S(2)}, u32[]{:S(2)}) %collective-permute-start.3) | collective-permute-done | bytes 1048608 | tf_op jit(solution)/shard_map/ppermute | solution.py:26
  131.7 4.8 %collective-permute-done.4 = f32[16,1,32,512]{3,2,1,0:T(8,128)S(1)} collective-permute-done((f32[16,1,32,512]{3,2,1,0:T(8,128)S(1)}, f32[16,1,32,512]{3,2,1,0:T(8,128)S(1)}, u32[]{:S(2)}, u32[]{:S(2)}) %collective-permute-start.4) | collective-permute-done | bytes 1048608 | tf_op jit(solution)/shard_map/ppermute | solution.py:23
  136.5 12.2 %multiply_reduce_fusion.2 = (f32[16]{0:T(128)S(1)}, f32[16,4,32,512]{3,2,1,0:T(8,128)}) fusion(f32[16,4,32,512]{3,2,1,0:T(8,128)S(1)} %multiply_add_fusion.1, f32[4,32,512]{2,1,0:T(8,128)S(1)} %get-tuple-element.35, f32[4,32,512]{2,1,0:T(8,128)S(1)} %get-tuple-element.24, f32[4,32,512]{2,1,0:T(8,128)S(1)} %get-tuple-element.34, ...), kind=kLoop, calls=%fused_computation.125 | loop fusion | flops 36700144 | bytes 13369408 | tf_op jit(solution)/shard_map/reduce_sum | solution.py:85
  148.7 0.0 copy-done.1
  148.7 37.5 %psum.45 = f32[16]{0:T(128)S(1)} all-reduce(f32[16]{0:T(128)S(1)} %get-tuple-element.9), channel_id=1, replica_groups=mesh['groups'=2,'day'=16] {'day'}, use_global_device_ids=true, to_apply=%region_7.8 | all-reduce | flops 16 | bytes 128 | tf_op jit(solution)/shard_map/psum | solution.py:107
  186.3 4.4 %multiply_reduce_fusion.1 = f32[16]{0:T(128)S(1)} fusion(f32[4,32,512]{2,1,0:T(8,128)S(1)} %get-tuple-element.31, f32[16,4,32,512]{3,2,1,0:T(8,128)} %get-tuple-element.12, f32[16,4,32,512]{3,2,1,0:T(8,128)} %get-tuple-element.10, f32[16]{0:T(128)S(1)} %div.46), kind=kLoop, calls=%fused_computation.123 | loop fusion | flops 5242864 | bytes 8650880 | tf_op jit(solution)/shard_map/reduce_sum | solution.py:85
  190.7 29.5 %psum.46 = f32[16]{0:T(128)S(1)} all-reduce(f32[16]{0:T(128)S(1)} %multiply_reduce_fusion.1), channel_id=1, replica_groups=mesh['groups'=2,'day'=16] {'day'}, use_global_device_ids=true, to_apply=%region_9.10 | all-reduce | flops 16 | bytes 128 | tf_op jit(solution)/shard_map/psum | solution.py:89
  220.2 6.4 %multiply_add_fusion = f32[16,4,32,512]{3,2,1,0:T(8,128)S(1)} fusion(f32[16,4,32,512]{3,2,1,0:T(8,128)} %copy-done.1, f32[16]{0:T(128)S(1)} %div.48, f32[4,32,512]{2,1,0:T(8,128)S(1)} %get-tuple-element.31, f32[16,4,32,512]{3,2,1,0:T(8,128)} %get-tuple-element.12, f32[16,4,32,512]{3,2,1,0:T(8,128)} %get-tuple-element.10, f32[16]{0:T(128)S(1)} %div.46), kind=kLoop, calls=%fused_computation.122 | loop fusion | flops 5242880 | bytes 17039488 | tf_op jit(solution)/shard_map/add | solution.py:113
  226.6 0.0 copy-start.2
  226.6 0.3 fusion.102
  226.9 0.1 collective-permute-start.5
  227.0 0.5 collective-permute-start.6
  227.5 11.8 %collective-permute-done.5 = f32[16,1,32,512]{3,2,1,0:T(8,128)S(1)} collective-permute-done((f32[16,1,32,512]{3,2,1,0:T(8,128)S(1)}, f32[16,1,32,512]{3,2,1,0:T(8,128)S(1)}, u32[]{:S(2)}, u32[]{:S(2)}) %collective-permute-start.5) | collective-permute-done | bytes 1048608 | tf_op jit(solution)/shard_map/ppermute | solution.py:26
  239.3 4.9 %collective-permute-done.6 = f32[16,1,32,512]{3,2,1,0:T(8,128)S(1)} collective-permute-done((f32[16,1,32,512]{3,2,1,0:T(8,128)S(1)}, f32[16,1,32,512]{3,2,1,0:T(8,128)S(1)}, u32[]{:S(2)}, u32[]{:S(2)}) %collective-permute-start.6) | collective-permute-done | bytes 1048608 | tf_op jit(solution)/shard_map/ppermute | solution.py:23
  244.2 0.0 copy-done.2
  244.2 11.4 %fusion.91 = f32[16]{0:T(128)S(1)} fusion(f32[16,4,32,512]{3,2,1,0:T(8,128)S(1)} %multiply_add_fusion, f32[16,1,32,512]{3,2,1,0:T(8,128)S(1)} %collective-permute-done.6, f32[16,1,32,512]{3,2,1,0:T(8,128)S(1)} %collective-permute-done.5, f32[4,32,512]{2,1,0:T(8,128)S(1)} %get-tuple-element.35, f32[4,32,512]{2,1,0:T(8,128)S(1)} %get-tuple-element.24, ...), kind=kLoop, calls=%fused_computation.133 | loop fusion | flops 36700144 | bytes 9175104 | tf_op jit(solution)/shard_map/reduce_sum | solution.py:85
  255.7 37.5 %psum.47 = f32[16]{0:T(128)S(1)} all-reduce(f32[16]{0:T(128)S(1)} %fusion.91), channel_id=1, replica_groups=mesh['groups'=2,'day'=16] {'day'}, use_global_device_ids=true, to_apply=%region_11.12 | all-reduce | flops 16 | bytes 128 | tf_op jit(solution)/shard_map/psum | solution.py:107
  293.2 6.5 %multiply_reduce_fusion = f32[4,32,512]{2,1,0:T(8,128)S(1)} fusion(f32[16,4,32,512]{3,2,1,0:T(8,128)} %copy-done.2, f32[16,4,32,512]{3,2,1,0:T(8,128)} %copy-done.1, s32[16,4,32,512]{3,2,1,0:T(8,128)} %param.4, f32[16]{0:T(128)S(1)} %div.49, f32[16]{0:T(128)S(1)} %div.46, f32[16]{0:T(128)S(1)} %div.43, f32[4,32,512]{2,1,0:T(8,128)S(1)} %get-tuple-element.31), kind=kLoop, calls=%fused_computation.121 | loop fusion | flops 11468800 | bytes 13107392 | tf_op jit(solution)/shard_map/reduce_sum | solution.py:115
  299.7 0.7 broadcast_multiply_fusion
  (6 shorter events, 0.0 us)
Async XLA Ops:
  0.0 9.9 %copy-start = (s32[16,4,32,512]{3,2,1,0:T(8,128)S(1)}, s32[16,4,32,512]{3,2,1,0:T(8,128)}, u32[]{:S(2)}) copy-start(s32[16,4,32,512]{3,2,1,0:T(8,128)} %param.4) | copy-start | bytes 12582916
  1.0 7.4 %collective-permute-start = (f32[1,32,512]{2,1,0:T(8,128)S(1)}, f32[1,32,512]{2,1,0:T(8,128)S(1)}, u32[]{:S(2)}, u32[]{:S(2)}) collective-permute-start(f32[1,32,512]{2,1,0:T(8,128)S(1)} %slice_bitcast_fusion.3), channel_id=1, source_target_pairs={{0,1},{1,2},{2,3},{3,4},{4,5},{5,6},{6,7},{7,8},{8,9},{9,10},{10,1... | collective-permute-start | bytes 196616 | tf_op jit(solution)/shard_map/ppermute | solution.py:14
  10.8 2.0 copy-start.3
  11.0 14.1 %collective-permute-start.1 = (f32[16,1,32,512]{3,2,1,0:T(8,128)S(1)}, f32[16,1,32,512]{3,2,1,0:T(8,128)S(1)}, u32[]{:S(2)}, u32[]{:S(2)}) collective-permute-start(f32[16,1,32,512]{3,2,1,0:T(8,128)S(1)} %get-tuple-element.18), channel_id=1, source_target_pairs={{1,0},{2,1},{3,2},{4,3},{5,4},{6,5},{7,6},{8,7},{9,8},{10,9},{11,1... | collective-permute-start | bytes 3145736 | tf_op jit(solution)/shard_map/ppermute | solution.py:26
  12.9 17.0 %collective-permute-start.2 = (f32[16,1,32,512]{3,2,1,0:T(8,128)S(1)}, f32[16,1,32,512]{3,2,1,0:T(8,128)S(1)}, u32[]{:S(2)}, u32[]{:S(2)}) collective-permute-start(f32[16,1,32,512]{3,2,1,0:T(8,128)S(1)} %get-tuple-element.19), channel_id=1, source_target_pairs={{0,1},{1,2},{2,3},{3,4},{4,5},{5,6},{6,7},{7,8},{8,9},{9,10},{10,1... | collective-permute-start | bytes 3145736 | tf_op jit(solution)/shard_map/ppermute | solution.py:23
  119.0 29.7 %copy-start.1 = (f32[16,4,32,512]{3,2,1,0:T(8,128)}, f32[16,4,32,512]{3,2,1,0:T(8,128)S(1)}, u32[]{:S(2)}) copy-start(f32[16,4,32,512]{3,2,1,0:T(8,128)S(1)} %multiply_add_fusion.1) | copy-start | bytes 12582916
  119.3 12.4 %collective-permute-start.3 = (f32[16,1,32,512]{3,2,1,0:T(8,128)S(1)}, f32[16,1,32,512]{3,2,1,0:T(8,128)S(1)}, u32[]{:S(2)}, u32[]{:S(2)}) collective-permute-start(f32[16,1,32,512]{3,2,1,0:T(8,128)S(1)} %get-tuple-element.16), channel_id=1, source_target_pairs={{1,0},{2,1},{3,2},{4,3},{5,4},{6,5},{7,6},{8,7},{9,8},{10,9},{11,1... | collective-permute-start | bytes 3145736 | tf_op jit(solution)/shard_map/ppermute | solution.py:26
  119.4 17.1 %collective-permute-start.4 = (f32[16,1,32,512]{3,2,1,0:T(8,128)S(1)}, f32[16,1,32,512]{3,2,1,0:T(8,128)S(1)}, u32[]{:S(2)}, u32[]{:S(2)}) collective-permute-start(f32[16,1,32,512]{3,2,1,0:T(8,128)S(1)} %get-tuple-element.17), channel_id=1, source_target_pairs={{0,1},{1,2},{2,3},{3,4},{4,5},{5,6},{6,7},{7,8},{8,9},{9,10},{10,1... | collective-permute-start | bytes 3145736 | tf_op jit(solution)/shard_map/ppermute | solution.py:23
  226.6 17.6 %copy-start.2 = (f32[16,4,32,512]{3,2,1,0:T(8,128)}, f32[16,4,32,512]{3,2,1,0:T(8,128)S(1)}, u32[]{:S(2)}) copy-start(f32[16,4,32,512]{3,2,1,0:T(8,128)S(1)} %multiply_add_fusion) | copy-start | bytes 12582916
  226.9 12.4 %collective-permute-start.5 = (f32[16,1,32,512]{3,2,1,0:T(8,128)S(1)}, f32[16,1,32,512]{3,2,1,0:T(8,128)S(1)}, u32[]{:S(2)}, u32[]{:S(2)}) collective-permute-start(f32[16,1,32,512]{3,2,1,0:T(8,128)S(1)} %get-tuple-element.14), channel_id=1, source_target_pairs={{1,0},{2,1},{3,2},{4,3},{5,4},{6,5},{7,6},{8,7},{9,8},{10,9},{11,1... | collective-permute-start | bytes 3145736 | tf_op jit(solution)/shard_map/ppermute | solution.py:26
  227.0 17.3 %collective-permute-start.6 = (f32[16,1,32,512]{3,2,1,0:T(8,128)S(1)}, f32[16,1,32,512]{3,2,1,0:T(8,128)S(1)}, u32[]{:S(2)}, u32[]{:S(2)}) collective-permute-start(f32[16,1,32,512]{3,2,1,0:T(8,128)S(1)} %get-tuple-element.15), channel_id=1, source_target_pairs={{0,1},{1,2},{2,3},{3,4},{4,5},{5,6},{6,7},{7,8},{8,9},{9,10},{10,1... | collective-permute-start | bytes 3145736 | tf_op jit(solution)/shard_map/ppermute | solution.py:23
where the time goes:
time: 301 us; the launch traced here: 300 us
  blocking collectives  170 us (56%)
  other arithmetic  71.1 us (24%)
  waiting for transfers between devices  53.6 us (18%)
  starting transfers between devices  3.38 us (1%)
    psum x3, blocking collectives, norm_sum(): return lax.psum(summed(residual, scaled), 'day')  94.5 us
    psum x2, blocking collectives, body(): step_len = norm_now / lax.psum(summed(direction, image), 'day')  75.1 us
    reduce_sum x5, other arithmetic, summed(): return jnp.sum(first * second, axis=(1, 2, 3))  47.6 us
    ppermute x3, waiting for transfers between devices, extended(): lax.ppermute(lax.slice_in_dim(block, 0, width, axis=dim), axis, backward)  35.7 us
    ppermute x3, waiting for transfers between devices, extended(): lax.ppermute(lax.slice_in_dim(block, block.shape[dim] - width, None, axis...  14.4 us
    add x2, other arithmetic, body(): direction = scaled + spread(norm_next / norm_now) * direction  11.1 us
    reduce_sum x1, other arithmetic, body(): return jnp.sum(signs * estimate, axis=0) / probes_n  6.5 us
  transfers between devices with their start and end apart: 7, of which 7 were waited for; matrix products, arithmetic and copies ran while one was open for 1% of the time, Pallas kernels for 0%

commit v1 on v0

--- a/solution.py
+++ b/solution.py
@@ -86,7 +86,7 @@
 
 
 def norm_sum(residual, scaled):
-    return lax.psum(summed(residual, scaled), "day")
+    return jnp.sum(lax.all_gather(summed(residual, scaled), "day"), axis=0)
 
 
 def body(couplings, probe_bits, land_mask):

time: 301 us -> 322 us (1.070)
  other arithmetic: 71.1 us -> 87.5 us
  local copies, waits for them, and re-layouts: 2.67 us -> 8.21 us
    unnamed x0 -> x3, blocking collectives: none -> 94.7 us
    psum x3 -> x0, blocking collectives: 94.5 us -> none  [norm_sum(): return lax.psum(summed(residual, scaled), 'day')]
    reduce_sum x5, other arithmetic: 47.6 us -> 63.1 us  [summed(): return jnp.sum(first * second, axis=(1, 2, 3))]
    unnamed x8 -> x43, local copies, waits for them, and re-layouts: 0.02 us -> 3.88 us
  transfers between devices with their start and end apart: 7 -> 7, of which waited for: 7 -> 7; matrix products, arithmetic and copies ran while one was open for 1% -> 2% of each run, Pallas kernels for 0% -> 0%
where the time goes in v1:
time: 322 us
  blocking collectives  170 us (53%)
  other arithmetic  87.5 us (27%)
  waiting for transfers between devices  51 us (16%)
  local copies, waits for them, and re-layouts  8.21 us (3%)
  starting transfers between devices  3.99 us (1%)
    unnamed x3, blocking collectives  94.7 us
    psum x2, blocking collectives, body(): step_len = norm_now / lax.psum(summed(direction, image), 'day')  75.2 us
    reduce_sum x5, other arithmetic, summed(): return jnp.sum(first * second, axis=(1, 2, 3))  63.1 us
    ppermute x3, waiting for transfers between devices, extended(): lax.ppermute(lax.slice_in_dim(block, 0, width, axis=dim), axis, backward)  34 us
    ppermute x3, waiting for transfers between devices, extended(): lax.ppermute(lax.slice_in_dim(block, block.shape[dim] - width, None, axis...  14.2 us
    add x2, other arithmetic, body(): direction = scaled + spread(norm_next / norm_now) * direction  11.1 us
    reduce_sum x1, other arithmetic, body(): return jnp.sum(signs * estimate, axis=0) / probes_n  6.5 us
  transfers between devices with their start and end apart: 7, of which 7 were waited for; matrix products, arithmetic and copies ran while one was open for 2% of the time, Pallas kernels for 0%

profile of v1, /device:TPU:0, one launch (start us, length us, event | category | flops | bytes accessed | tf_op | source)
XLA Modules:
  0.0 321.5 jit_solution(9494044875494389691)
XLA Ops:
  0.0 1.0 slice_bitcast_fusion.3
  1.0 0.5 collective-permute-start
  1.5 1.2 fusion.93
  2.7 0.0 copy-start.15
  2.7 0.6 copy-done.15
  3.3 0.0 copy-done.16
  3.3 1.3 bitcast_multiply_fusion.3
  4.7 0.9 slice_bitcast_fusion.2
  5.6 2.8 collective-permute-done
  8.4 1.5 pad_maximum_fusion.6
  9.9 0.9 convert_divide_fusion
  10.9 1.9 copy-done.3
  12.8 1.6 fusion.104
  14.4 2.4 collective-permute-start.1
  16.8 0.6 dynamic-slice
  18.0 1.1 slice_bitcast_fusion.1
  19.1 10.3 %collective-permute-done.1 = f32[16,1,32,512]{3,2,1,0:T(8,128)} collective-permute-done((f32[16,1,32,512]{3,2,1,0:T(8,128)}, f32[16,1,32,512]{3,2,1,0:T(8,128)}, u32[]{:S(2)}, u32[]{:S(2)}) %collective-permute-start.1) | collective-permute-done | bytes 1048608 | tf_op jit(solution)/shard_map/ppermute | solution.py:26
  29.5 4.7 %collective-permute-done.2 = f32[16,1,32,512]{3,2,1,0:T(8,128)} collective-permute-done((f32[16,1,32,512]{3,2,1,0:T(8,128)}, f32[16,1,32,512]{3,2,1,0:T(8,128)}, u32[]{:S(2)}, u32[]{:S(2)}) %collective-permute-start.2) | collective-permute-done | bytes 1048608 | tf_op jit(solution)/shard_map/ppermute | solution.py:23
  34.2 28.3 %multiply_reduce_fusion.4 = (f32[16]{0:T(128)S(1)}, f32[16]{0:T(128)S(1)}, f32[16,4,32,512]{3,2,1,0:T(8,128)}) fusion(f32[4,32,512]{2,1,0:T(8,128)S(1)} %get-tuple-element.31, s32[16,4,32,512]{3,2,1,0:T(8,128)} %param.4, f32[16,4,32,512]{3,2,1,0:T(8,128)} %copy-done.3, f32[4,32,512]{2,1,0:T(8,128)S(1)} %get-tuple-element.35, ...), kind=kLoop, calls=%fused_computation.129 | loop fusion | flops 42991584 | bytes 17825920 | tf_op jit(solution)/shard_map/reduce_sum | solution.py:85
  62.5 0.2 dynamic-update-slice
  62.8 35.4 %all-reduce.39 = (f32[256]{0:T(256)S(1)}, f32[16]{0:T(128)S(1)}) all-reduce(f32[256]{0:T(256)S(1)} %dynamic-update-slice, f32[16]{0:T(128)S(1)} %get-tuple-element.5), channel_id=2, replica_groups=mesh['groups'=2,'day'=16] {'day'}, use_global_device_ids=true, to_apply=%add.36 | all-reduce | flops 272 | bytes 2176
  98.1 0.1 reshape.23
  98.2 6.6 %multiply_reduce_fusion.3 = (f32[16]{0:T(128)S(1)}, f32[16,4,32,512]{3,2,1,0:T(8,128)}) fusion(f32[4,32,512]{2,1,0:T(8,128)S(1)} %get-tuple-element.31, f32[16,4,32,512]{3,2,1,0:T(8,128)} %get-tuple-element.13, f32[16]{0:T(128)S(1)} %div.51, s32[16,4,32,512]{3,2,1,0:T(8,128)} %param.4), kind=kLoop, calls=%fused_computation.127 | loop fusion | flops 8388592 | bytes 12845184 | tf_op jit(solution)/shard_map/reduce_sum | solution.py:85
  104.9 0.2 dynamic-update-slice.1
  105.1 29.6 %all-reduce.37 = f32[256]{0:T(256)S(1)} all-reduce(f32[256]{0:T(256)S(1)} %dynamic-update-slice.1), channel_id=3, replica_groups=mesh['groups'=2,'day'=16] {'day'}, use_global_device_ids=true, to_apply=%add.37 | all-reduce | flops 256 | bytes 2048
  134.7 0.1 reshape.24
  134.8 4.6 %multiply_add_fusion.1 = f32[16,4,32,512]{3,2,1,0:T(8,128)S(1)} fusion(f32[16,4,32,512]{3,2,1,0:T(8,128)} %get-tuple-element.12, f32[16]{0:T(128)S(1)} %div.53, f32[4,32,512]{2,1,0:T(8,128)S(1)} %get-tuple-element.31, s32[16,4,32,512]{3,2,1,0:T(8,128)} %param.4), kind=kLoop, calls=%fused_computation.126 | loop fusion | flops 7340032 | bytes 12845120 | tf_op jit(solution)/shard_map/add | solution.py:113
  139.5 0.3 fusion.103
  139.8 0.1 collective-permute-start.3
  139.9 0.5 collective-permute-start.4
  140.4 11.8 %collective-permute-done.3 = f32[16,1,32,512]{3,2,1,0:T(8,128)S(1)} collective-permute-done((f32[16,1,32,512]{3,2,1,0:T(8,128)S(1)}, f32[16,1,32,512]{3,2,1,0:T(8,128)S(1)}, u32[]{:S(2)}, u32[]{:S(2)}) %collective-permute-start.3) | collective-permute-done | bytes 1048608 | tf_op jit(solution)/shard_map/ppermute | solution.py:26
  152.2 4.8 %collective-permute-done.4 = f32[16,1,32,512]{3,2,1,0:T(8,128)S(1)} collective-permute-done((f32[16,1,32,512]{3,2,1,0:T(8,128)S(1)}, f32[16,1,32,512]{3,2,1,0:T(8,128)S(1)}, u32[]{:S(2)}, u32[]{:S(2)}) %collective-permute-start.4) | collective-permute-done | bytes 1048608 | tf_op jit(solution)/shard_map/ppermute | solution.py:23
  157.0 12.3 %multiply_reduce_fusion.2 = (f32[16]{0:T(128)S(1)}, f32[16,4,32,512]{3,2,1,0:T(8,128)}) fusion(f32[16,4,32,512]{3,2,1,0:T(8,128)S(1)} %multiply_add_fusion.1, f32[4,32,512]{2,1,0:T(8,128)S(1)} %get-tuple-element.35, f32[4,32,512]{2,1,0:T(8,128)S(1)} %copy-done.12, f32[4,32,512]{2,1,0:T(8,128)S(1)} %get-tuple-element.34, f32[4,32,512]{2,1,0:T(8,128)S(1)} %copy-done.10, ...), kind=kLoop, calls=%fused_computation.125 | loop fusion | flops 36700144 | bytes 13369408 | tf_op jit(solution)/shard_map/reduce_sum | solution.py:85
  169.3 37.5 %psum.22 = f32[16]{0:T(128)S(1)} all-reduce(f32[16]{0:T(128)S(1)} %get-tuple-element.9), channel_id=1, replica_groups=mesh['groups'=2,'day'=16] {'day'}, use_global_device_ids=true, to_apply=%region_7.8 | all-reduce | flops 16 | bytes 128 | tf_op jit(solution)/shard_map/psum | solution.py:107
  206.8 4.4 %multiply_reduce_fusion.1 = f32[16]{0:T(128)S(1)} fusion(f32[4,32,512]{2,1,0:T(8,128)S(1)} %get-tuple-element.31, f32[16,4,32,512]{3,2,1,0:T(8,128)} %get-tuple-element.12, f32[16,4,32,512]{3,2,1,0:T(8,128)} %get-tuple-element.10, f32[16]{0:T(128)S(1)} %div.54), kind=kLoop, calls=%fused_computation.123 | loop fusion | flops 5242864 | bytes 8650880 | tf_op jit(solution)/shard_map/reduce_sum | solution.py:85
  211.3 0.2 dynamic-update-slice.2
  211.5 29.7 %all-reduce.38 = f32[256]{0:T(256)S(1)} all-reduce(f32[256]{0:T(256)S(1)} %dynamic-update-slice.2), channel_id=4, replica_groups=mesh['groups'=2,'day'=16] {'day'}, use_global_device_ids=true, to_apply=%add.38 | all-reduce | flops 256 | bytes 2048
  241.2 0.1 reshape.25
  241.3 6.4 %multiply_add_fusion = f32[16,4,32,512]{3,2,1,0:T(8,128)S(1)} fusion(f32[16,4,32,512]{3,2,1,0:T(8,128)} %copy-done.1, f32[16]{0:T(128)S(1)} %div.56, f32[4,32,512]{2,1,0:T(8,128)S(1)} %get-tuple-element.31, f32[16,4,32,512]{3,2,1,0:T(8,128)} %get-tuple-element.12, f32[16,4,32,512]{3,2,1,0:T(8,128)} %get-tuple-element.10, f32[16]{0:T(128)S(1)} %div.54), kind=kLoop, calls=%fused_computation.122 | loop fusion | flops 5242880 | bytes 17039488 | tf_op jit(solution)/shard_map/add | solution.py:113
  247.7 0.3 fusion.102
  248.0 0.1 collective-permute-start.5
  248.1 0.5 collective-permute-start.6
  248.6 11.8 %collective-permute-done.5 = f32[16,1,32,512]{3,2,1,0:T(8,128)S(1)} collective-permute-done((f32[16,1,32,512]{3,2,1,0:T(8,128)S(1)}, f32[16,1,32,512]{3,2,1,0:T(8,128)S(1)}, u32[]{:S(2)}, u32[]{:S(2)}) %collective-permute-start.5) | collective-permute-done | bytes 1048608 | tf_op jit(solution)/shard_map/ppermute | solution.py:26
  260.4 4.8 %collective-permute-done.6 = f32[16,1,32,512]{3,2,1,0:T(8,128)S(1)} collective-permute-done((f32[16,1,32,512]{3,2,1,0:T(8,128)S(1)}, f32[16,1,32,512]{3,2,1,0:T(8,128)S(1)}, u32[]{:S(2)}, u32[]{:S(2)}) %collective-permute-start.6) | collective-permute-done | bytes 1048608 | tf_op jit(solution)/shard_map/ppermute | solution.py:23
  265.1 11.4 %fusion.91 = f32[16]{0:T(128)S(1)} fusion(f32[16,4,32,512]{3,2,1,0:T(8,128)S(1)} %multiply_add_fusion, f32[16,1,32,512]{3,2,1,0:T(8,128)S(1)} %collective-permute-done.6, f32[16,1,32,512]{3,2,1,0:T(8,128)S(1)} %collective-permute-done.5, f32[4,32,512]{2,1,0:T(8,128)S(1)} %get-tuple-element.35, f32[4,32,512]{2,1,0:T(8,128)S(1)} %copy-done.12, ...), kind=kLoop, calls=%fused_computation.133 | loop fusion | flops 36700144 | bytes 9175104 | tf_op jit(solution)/shard_map/reduce_sum | solution.py:85
  276.6 37.7 %psum.23 = f32[16]{0:T(128)S(1)} all-reduce(f32[16]{0:T(128)S(1)} %fusion.91), channel_id=1, replica_groups=mesh['groups'=2,'day'=16] {'day'}, use_global_device_ids=true, to_apply=%region_11.12 | all-reduce | flops 16 | bytes 128 | tf_op jit(solution)/shard_map/psum | solution.py:107
  314.3 6.5 %multiply_reduce_fusion = f32[4,32,512]{2,1,0:T(8,128)S(1)} fusion(f32[16,4,32,512]{3,2,1,0:T(8,128)} %copy-done.2, f32[16,4,32,512]{3,2,1,0:T(8,128)} %copy-done.1, s32[16,4,32,512]{3,2,1,0:T(8,128)} %param.4, f32[16]{0:T(128)S(1)} %div.57, f32[16]{0:T(128)S(1)} %div.54, f32[16]{0:T(128)S(1)} %div.51, f32[4,32,512]{2,1,0:T(8,128)S(1)} %get-tuple-element.31), kind=kLoop, calls=%fused_computation.121 | loop fusion | flops 11468800 | bytes 13107392 | tf_op jit(solution)/shard_map/reduce_sum | solution.py:115
  320.8 0.7 broadcast_multiply_fusion
  (45 shorter events, 0.2 us)
Async XLA Ops:
  0.0 9.9 %copy-start = (s32[16,4,32,512]{3,2,1,0:T(8,128)S(1)}, s32[16,4,32,512]{3,2,1,0:T(8,128)}, u32[]{:S(2)}) copy-start(s32[16,4,32,512]{3,2,1,0:T(8,128)} %param.4) | copy-start | bytes 12582916
  1.0 7.4 %collective-permute-start = (f32[1,32,512]{2,1,0:T(8,128)S(1)}, f32[1,32,512]{2,1,0:T(8,128)S(1)}, u32[]{:S(2)}, u32[]{:S(2)}) collective-permute-start(f32[1,32,512]{2,1,0:T(8,128)S(1)} %slice_bitcast_fusion.3), channel_id=1, source_target_pairs={{0,1},{1,2},{2,3},{3,4},{4,5},{5,6},{6,7},{7,8},{8,9},{9,10},{10,1... | collective-permute-start | bytes 196616 | tf_op jit(solution)/shard_map/ppermute | solution.py:14
  2.7 0.6 copy-start.15
  2.7 0.6 copy-start.16
  10.8 1.9 copy-start.3
  12.8 4.1 %copy-start.17 = (u32[32]{0:T(128)S(1)}, u32[32]{0:T(128)}, u32[]{:S(2)}) copy-start(u32[32]{0:T(128)} %constant.94) | copy-start | bytes 388
  12.8 5.2 %copy-start.4 = (f32[6,4,32,512]{3,2,1,0:T(8,128)S(1)}, f32[6,4,32,512]{3,2,1,0:T(8,128)}, u32[]{:S(2)}) copy-start(f32[6,4,32,512]{3,2,1,0:T(8,128)} %param.3) | copy-start | bytes 4718596
  14.4 15.1 %collective-permute-start.1 = (f32[16,1,32,512]{3,2,1,0:T(8,128)}, f32[16,1,32,512]{3,2,1,0:T(8,128)}, u32[]{:S(2)}, u32[]{:S(2)}) collective-permute-start(f32[16,1,32,512]{3,2,1,0:T(8,128)} %get-tuple-element.18), channel_id=1, source_target_pairs={{1,0},{2,1},{3,2},{4,3},{5,4},{6,5},{7,6},{8,7},{9,8},{10,9},{11,1... | collective-permute-start | bytes 3145736 | tf_op jit(solution)/shard_map/ppermute | solution.py:26
  16.8 17.3 %collective-permute-start.2 = (f32[16,1,32,512]{3,2,1,0:T(8,128)}, f32[16,1,32,512]{3,2,1,0:T(8,128)}, u32[]{:S(2)}, u32[]{:S(2)}) collective-permute-start(f32[16,1,32,512]{3,2,1,0:T(8,128)} %get-tuple-element.19), channel_id=1, source_target_pairs={{0,1},{1,2},{2,3},{3,4},{4,5},{5,6},{6,7},{7,8},{8,9},{9,10},{10,1... | collective-permute-start | bytes 3145736 | tf_op jit(solution)/shard_map/ppermute | solution.py:23
  19.1 43.4 %copy-start.5 = (f32[4,32,512]{2,1,0:T(8,128)}, f32[4,32,512]{2,1,0:T(8,128)S(1)}, u32[]{:S(2)}) copy-start(f32[4,32,512]{2,1,0:T(8,128)S(1)} %get-tuple-element.21) | copy-start | bytes 786436
  19.1 43.4 %copy-start.7 = (f32[4,32,512]{2,1,0:T(8,128)}, f32[4,32,512]{2,1,0:T(8,128)S(1)}, u32[]{:S(2)}) copy-start(f32[4,32,512]{2,1,0:T(8,128)S(1)} %get-tuple-element.22) | copy-start | bytes 786436
  19.1 43.4 %copy-start.9 = (f32[4,32,512]{2,1,0:T(8,128)}, f32[4,32,512]{2,1,0:T(8,128)S(1)}, u32[]{:S(2)}) copy-start(f32[4,32,512]{2,1,0:T(8,128)S(1)} %get-tuple-element.23) | copy-start | bytes 786436
  19.1 43.4 %copy-start.11 = (f32[4,32,512]{2,1,0:T(8,128)}, f32[4,32,512]{2,1,0:T(8,128)S(1)}, u32[]{:S(2)}) copy-start(f32[4,32,512]{2,1,0:T(8,128)S(1)} %get-tuple-element.24) | copy-start | bytes 786436
  19.1 43.4 %copy-start.13 = (f32[4,32,512]{2,1,0:T(8,128)}, f32[4,32,512]{2,1,0:T(8,128)S(1)}, u32[]{:S(2)}) copy-start(f32[4,32,512]{2,1,0:T(8,128)S(1)} %get-tuple-element.25) | copy-start | bytes 786436
  139.5 29.8 %copy-start.1 = (f32[16,4,32,512]{3,2,1,0:T(8,128)}, f32[16,4,32,512]{3,2,1,0:T(8,128)S(1)}, u32[]{:S(2)}) copy-start(f32[16,4,32,512]{3,2,1,0:T(8,128)S(1)} %multiply_add_fusion.1) | copy-start | bytes 12582916
  139.5 17.5 %copy-start.6 = (f32[4,32,512]{2,1,0:T(8,128)S(1)}, f32[4,32,512]{2,1,0:T(8,128)}, u32[]{:S(2)}) copy-start(f32[4,32,512]{2,1,0:T(8,128)} %copy-done.5) | copy-start | bytes 786436
  139.5 17.5 %copy-start.8 = (f32[4,32,512]{2,1,0:T(8,128)S(1)}, f32[4,32,512]{2,1,0:T(8,128)}, u32[]{:S(2)}) copy-start(f32[4,32,512]{2,1,0:T(8,128)} %copy-done.7) | copy-start | bytes 786436
  139.5 17.5 %copy-start.10 = (f32[4,32,512]{2,1,0:T(8,128)S(1)}, f32[4,32,512]{2,1,0:T(8,128)}, u32[]{:S(2)}) copy-start(f32[4,32,512]{2,1,0:T(8,128)} %copy-done.9) | copy-start | bytes 786436
  139.5 17.5 %copy-start.12 = (f32[4,32,512]{2,1,0:T(8,128)S(1)}, f32[4,32,512]{2,1,0:T(8,128)}, u32[]{:S(2)}) copy-start(f32[4,32,512]{2,1,0:T(8,128)} %copy-done.11) | copy-start | bytes 786436
  139.5 17.5 %copy-start.14 = (f32[4,32,512]{2,1,0:T(8,128)S(1)}, f32[4,32,512]{2,1,0:T(8,128)}, u32[]{:S(2)}) copy-start(f32[4,32,512]{2,1,0:T(8,128)} %copy-done.13) | copy-start | bytes 786436
  139.8 12.4 %collective-permute-start.3 = (f32[16,1,32,512]{3,2,1,0:T(8,128)S(1)}, f32[16,1,32,512]{3,2,1,0:T(8,128)S(1)}, u32[]{:S(2)}, u32[]{:S(2)}) collective-permute-start(f32[16,1,32,512]{3,2,1,0:T(8,128)S(1)} %get-tuple-element.16), channel_id=1, source_target_pairs={{1,0},{2,1},{3,2},{4,3},{5,4},{6,5},{7,6},{8,7},{9,8},{10,9},{11,1... | collective-permute-start | bytes 3145736 | tf_op jit(solution)/shard_map/ppermute | solution.py:26
  139.9 17.1 %collective-permute-start.4 = (f32[16,1,32,512]{3,2,1,0:T(8,128)S(1)}, f32[16,1,32,512]{3,2,1,0:T(8,128)S(1)}, u32[]{:S(2)}, u32[]{:S(2)}) collective-permute-start(f32[16,1,32,512]{3,2,1,0:T(8,128)S(1)} %get-tuple-element.17), channel_id=1, source_target_pairs={{0,1},{1,2},{2,3},{3,4},{4,5},{5,6},{6,7},{7,8},{8,9},{9,10},{10,1... | collective-permute-start | bytes 3145736 | tf_op jit(solution)/shard_map/ppermute | solution.py:23
  247.7 17.4 %copy-start.2 = (f32[16,4,32,512]{3,2,1,0:T(8,128)}, f32[16,4,32,512]{3,2,1,0:T(8,128)S(1)}, u32[]{:S(2)}) copy-start(f32[16,4,32,512]{3,2,1,0:T(8,128)S(1)} %multiply_add_fusion) | copy-start | bytes 12582916
  248.0 12.4 %collective-permute-start.5 = (f32[16,1,32,512]{3,2,1,0:T(8,128)S(1)}, f32[16,1,32,512]{3,2,1,0:T(8,128)S(1)}, u32[]{:S(2)}, u32[]{:S(2)}) collective-permute-start(f32[16,1,32,512]{3,2,1,0:T(8,128)S(1)} %get-tuple-element.14), channel_id=1, source_target_pairs={{1,0},{2,1},{3,2},{4,3},{5,4},{6,5},{7,6},{8,7},{9,8},{10,9},{11,1... | collective-permute-start | bytes 3145736 | tf_op jit(solution)/shard_map/ppermute | solution.py:26
  248.1 17.1 %collective-permute-start.6 = (f32[16,1,32,512]{3,2,1,0:T(8,128)S(1)}, f32[16,1,32,512]{3,2,1,0:T(8,128)S(1)}, u32[]{:S(2)}, u32[]{:S(2)}) collective-permute-start(f32[16,1,32,512]{3,2,1,0:T(8,128)S(1)} %get-tuple-element.15), channel_id=1, source_target_pairs={{0,1},{1,2},{2,3},{3,4},{4,5},{5,6},{6,7},{7,8},{8,9},{9,10},{10,1... | collective-permute-start | bytes 3145736 | tf_op jit(solution)/shard_map/ppermute | solution.py:23
